TPU v7x, 512 devices: a whole 4x4x16 slice. The times are simulated.
512 devices in a mesh: gx: 32 (over z, core), gy: 16 (over y, x).
Axes of the slice: x: 4, y: 4, z: 16, core: 2. Of those that a mesh axis runs over, the one named last changes fastest.
Arguments:
- tokens: bfloat16 [8192, 2048], P('gx'), may hold values from -6 to 6
- lengths: int32 [4], replicated, may hold values from 1 to 4096, 8192 in all
- adapter_of_request: int32 [4], replicated, may hold values from 0 to 15
- adapter_storage_slot: int32 [16], replicated, may hold values from 0 to 15, each once
- page_cache_slot: int32 [1024], P('gx'), may hold values from 0 to 1023, as said below
- query_key_value_weight: bfloat16 [2048, 16, 384], P(None, 'gy'), may hold values from -4 to 4
- adapter_down_maps: bfloat16 [16, 2048, 48], P('gy'), may hold values from -0.125 to 0.125
- adapter_up_maps: bfloat16 [16, 3, 16, 16, 128], P(None, None, None, 'gy'), may hold values from -1.5 to 1.5
- query_norm_gain: float32 [16, 128], P('gy'), may hold values from 0.25 to 1.75
- key_norm_gain: float32 [16, 128], P('gy'), may hold values from 0.25 to 1.75
- output_weight: bfloat16 [16, 128, 2048], P('gy'), may hold values from -0.125 to 0.125
- post_norm_gain: float32 [2048], replicated, may hold values from 0.25 to 1.75
Outputs:
- mixed: bfloat16 [8192, 2048], P('gx')
- kv_cache: bfloat16 [1024, 8, 16, 256], P('gx', None, 'gy')
Inputs may be any that keep to these rules, and one draw needn't show every extreme that they name: `page_cache_slot`: each slot appears once; the 32 pages of the tokens of one index of gx have exactly 1 slot among the 32 slots held by each index k of gx (slots k * 32 onward).
All inputs are finite; a program needn't handle non-finite values.
Results may differ from a plain program's by a relative error of at most 0.017.
Values may be sent and summed in bfloat16 or wider, within the bound.
No kernel may reach another device: no remote copies, remote signals or barrier semaphores. Data moves between devices by JAX's collectives and lax.ppermute only.
A program may use at most 64 MiB of HBM per device.

v0:
```python
import jax
import jax.numpy as jnp
from jax import lax
from jax.sharding import PartitionSpec as P

MODEL_WIDTH = 2048
HEAD_SIZE = 128
ADAPTER_RANK = 16
PAGE = 8


def request_of(rows, ends):
    return jnp.sum((ends[None, :] <= rows[:, None]).astype(jnp.int32), axis=1)


def lookup(index, table):
    match = index[:, None] == jnp.arange(table.shape[0])[None, :]
    return jnp.sum(jnp.where(match, table[None, :], 0), axis=1)


def rotate(values, positions):
    half = values.shape[-1] // 2
    freq = 500000.0 ** (-(jnp.arange(half).astype(jnp.float32) * 2.0) / values.shape[-1])
    angle = positions.astype(jnp.float32)[:, None] * freq[None, :]
    cosine = jnp.cos(angle)[:, None, :]
    sine = jnp.sin(angle)[:, None, :]
    first = values[..., :half]
    second = values[..., half:]
    return jnp.concatenate(
        [first * cosine - second * sine, second * cosine + first * sine], axis=-1
    )


def shards(
    tokens,
    lengths,
    adapter_of_request,
    adapter_storage_slot,
    page_cache_slot,
    query_key_value_weight,
    adapter_down_maps,
    adapter_up_maps,
    query_norm_gain,
    key_norm_gain,
    output_weight,
    post_norm_gain,
):
    count = tokens.shape[0]
    group = lax.axis_index("gx")
    member = lax.axis_index("gy")
    rows = group * count + jnp.arange(count)
    ends = jnp.cumsum(lengths)
    starts = ends - lengths
    request = request_of(rows, ends)
    positions = rows - lookup(request, starts)
    slots = lookup(lookup(request, adapter_of_request), adapter_storage_slot)
    resident_count = adapter_down_maps.shape[0]
    held = member * resident_count + jnp.arange(resident_count)
    reduced_rows = jnp.einsum(
        "zm,ump->zup", tokens, adapter_down_maps, preferred_element_type=jnp.float32
    )
    chosen = (slots[:, None] == held[None, :]).astype(jnp.float32)
    partial_low = jnp.sum(chosen[:, :, None] * reduced_rows, axis=1)
    low = lax.psum(partial_low.astype(jnp.bfloat16), "gy")
    adapter_count_total = adapter_up_maps.shape[0]
    selector = (slots[:, None] == jnp.arange(adapter_count_total)[None, :]).astype(jnp.bfloat16)
    expanded_rows = selector[:, :, None, None] * low.reshape(count, 1, 3, ADAPTER_RANK)
    adapter_update = jnp.einsum(
        "dzqi,zqibj->dqbj", expanded_rows, adapter_up_maps, preferred_element_type=jnp.float32
    )
    base = jnp.einsum(
        "td,dhe->the", tokens, query_key_value_weight, preferred_element_type=jnp.float32
    )
    query = base[..., :HEAD_SIZE] + adapter_update[:, 0]
    key_raw = base[..., HEAD_SIZE : 2 * HEAD_SIZE] + adapter_update[:, 1]
    value = base[..., 2 * HEAD_SIZE :] + adapter_update[:, 2]
    query_sq, key_sq = lax.psum(
        (jnp.sum(query * query, axis=(1, 2)), jnp.sum(key_raw * key_raw, axis=(1, 2))), "gy"
    )
    query_n = (
        query * lax.rsqrt(query_sq / MODEL_WIDTH + 1e-06)[:, None, None] * query_norm_gain[None]
    )
    key_n = key_raw * lax.rsqrt(key_sq / MODEL_WIDTH + 1e-06)[:, None, None] * key_norm_gain[None]
    query_b = rotate(query_n, positions).astype(jnp.bfloat16)
    key_b = rotate(key_n, positions).astype(jnp.bfloat16)
    value_b = value.astype(jnp.bfloat16)
    heads_here = query_key_value_weight.shape[1]
    pages_here = count // PAGE
    pages = jnp.concatenate([key_b, value_b], axis=-1).reshape(
        pages_here, PAGE, heads_here, 2 * HEAD_SIZE
    )
    order = jnp.argsort(page_cache_slot)
    got_pages, got_slots = (
        lax.all_to_all(pages[order], "gx", split_axis=0, concat_axis=0, tiled=True),
        lax.all_to_all(page_cache_slot[order], "gx", split_axis=0, concat_axis=0, tiled=True),
    )
    kv_cache = got_pages[jnp.argsort(got_slots)]
    scale = HEAD_SIZE ** (-0.5)

    def attend(carry, key_vectors, values, key_rows):
        best, total, accum = carry
        key_request = request_of(key_rows, ends)
        scores = (
            jnp.einsum("the,khe->htk", query_b, key_vectors, preferred_element_type=jnp.float32)
            * scale
        )
        allowed = (request[:, None] == key_request[None, :]) & (key_rows[None, :] <= rows[:, None])
        masked = jnp.where(allowed[None], scores, -1e30)
        new_best = jnp.maximum(best, jnp.max(masked, axis=-1))
        weights = jnp.where(allowed[None], jnp.exp(scores - new_best[..., None]), 0.0)
        factor = jnp.exp(best - new_best)
        total = total * factor + jnp.sum(weights, axis=-1)
        update = jnp.einsum(
            "htk,khe->hte", weights.astype(jnp.bfloat16), values, preferred_element_type=jnp.float32
        )
        accum = accum * factor[..., None] + update
        return (new_best, total, accum)

    initial = (
        jnp.full((heads_here, count), -1e30, jnp.float32),
        jnp.zeros((heads_here, count), jnp.float32),
        jnp.zeros((heads_here, count, HEAD_SIZE), jnp.float32),
    )
    key_vectors = lax.all_gather(key_b, "gx", axis=0, tiled=True)
    values = lax.all_gather(value_b, "gx", axis=0, tiled=True)
    size = key_vectors.shape[0]
    block = 512

    def one_block(index, state):
        begin = index * block
        key_part = lax.dynamic_slice_in_dim(key_vectors, begin, block, 0)
        value_part = lax.dynamic_slice_in_dim(values, begin, block, 0)
        key_rows = begin + jnp.arange(block)
        return attend(state, key_part, value_part, key_rows)

    best, total, accum = lax.fori_loop(0, size // block, one_block, initial)
    attn = (accum / total[..., None]).astype(jnp.bfloat16)
    partial_out = jnp.einsum("hte,hed->td", attn, output_weight, preferred_element_type=jnp.float32)
    output = lax.psum(partial_out.astype(jnp.bfloat16), "gy").astype(jnp.float32)
    normed = (
        output
        * lax.rsqrt(jnp.mean(output * output, axis=1) + 1e-06)[:, None]
        * post_norm_gain[None, :]
    )
    mixed = (tokens.astype(jnp.float32) + normed).astype(jnp.bfloat16)
    return (mixed, kv_cache)


def solution(mesh):
    return jax.shard_map(
        shards,
        mesh=mesh,
        in_specs=(
            P("gx", None),
            P(),
            P(),
            P(),
            P("gx"),
            P(None, "gy", None),
            P("gy", None, None),
            P(None, None, None, "gy", None),
            P("gy", None),
            P("gy", None),
            P("gy", None, None),
            P(),
        ),
        out_specs=(P("gx", None), P("gx", None, "gy", None)),
        check_vma=False,
    )
```

profile of v0, /device:TPU:32, one launch (start us, length us, event | category | flops | bytes accessed | tf_op | source)
XLA Modules:
  0.0 445.1 jit_solution(11517718805805738873)
XLA Ops:
  10.4 1.7 fusion.33
  12.2 74.6 %psum.28 = bf16[256,3,16]{0,2,1:T(8,128)(2,1)S(1)} all-reduce(bf16[256,3,16]{0,2,1:T(8,128)(2,1)S(1)} %bitcast.114), channel_id=1, replica_groups=mesh['gx'=32,'gy'=16] {'gy'}, use_global_device_ids=true, to_apply=%region_4.5 | all-reduce | flops 12288 | bytes 49152 | tf_op jit(solution)/shard_map/psum | solution.py:64
  86.8 1.9 fusion.30
  89.2 35.5 %all-reduce = (f32[256]{0:T(256)S(1)}, f32[256]{0:T(256)S(1)}) all-reduce(f32[256]{0:T(256)S(1)} %get-tuple-element.231, f32[256]{0:T(256)S(1)} %get-tuple-element.230), channel_id=1, replica_groups=mesh['gx'=32,'gy'=16] {'gy'}, use_global_device_ids=true, to_apply=%region_6.7 | all-reduce | flops 512 | bytes 4096 | tf_op jit(solution)/shard_map/psum | solution.py:77
  127.7 71.4 %all-gather.3.cloned.1.call-done = bf16[8192,1,128]{2,0,1:T(8,128)(2,1)} async-done(((bf16[256,1,128]{2,0,1:T(8,128)(2,1)}), bf16[8192,1,128]{2,0,1:T(8,128)(2,1)}) %all-gather.3.cloned.1.call-update) | async-done | bytes 2097168 | tf_op jit(solution)/shard_map/all_gather | solution.py:124
  199.1 71.5 %all-gather.5.cloned.1.call-done = bf16[8192,1,128]{2,0,1:T(8,128)(2,1)} async-done(((bf16[256,1,128]{2,0,1:T(8,128)(2,1)}), bf16[8192,1,128]{2,0,1:T(8,128)(2,1)}) %all-gather.5.cloned.1.call-update) | async-done | bytes 2097168 | tf_op jit(solution)/shard_map/all_gather | solution.py:125
  270.6 47.3 %while.18 = (s32[]{:T(128)}, f32[1,256]{1,0:T(1,128)S(1)}, f32[1,256]{1,0:T(1,128)S(1)}, f32[1,256,128]{2,1,0:T(8,128)S(1)}, s32[256]{0:T(256)S(1)}, /*index=5*/...) while((s32[]{:T(128)}, f32[1,256]{1,0:T(1,128)S(1)}, ...), condition=%wide.region_14.15_spmd.clone, body=%wide.region_10.14_spmd.clone.sunk | while | flops 69574144 | bytes 2204895 | solution.py:136
  275.2 1.4 fusion.75
  281.1 1.4 fusion.75
  287.0 1.4 fusion.75
  292.9 1.4 fusion.75
  304.7 1.4 fusion.75
  310.6 1.4 fusion.75
  316.5 1.4 fusion.75
  317.9 1.5 convolution_convert_fusion
  319.4 1.7 sort.31
  322.5 8.5 %all-to-all-start.1 = ((s32[32,1,1]{2,1,0:T(1,128)}), s32[32,1,1]{2,1,0:T(1,128)S(1)}, u32[]{:S(2)}, u32[]{:S(2)}) async-start(s32[32,1,1]{2,1,0:T(1,128)} %copy.31), calls=%async_computation.1 | async-start | bytes 32768 | tf_op jit(solution)/shard_map/all_to_all | solution.py:95
  332.4 9.8 %all-to-all-done.1 = s32[32,1,1]{2,1,0:T(1,128)S(1)} async-done(((s32[32,1,1]{2,1,0:T(1,128)}), s32[32,1,1]{2,1,0:T(1,128)S(1)}, u32[]{:S(2)}, u32[]{:S(2)}) %all-to-all-start.1) | async-done | bytes 160 | tf_op jit(solution)/shard_map/all_to_all | solution.py:95
  342.2 5.0 %all-to-all-start = ((bf16[32,8,1,256]{3,1,2,0:T(8,128)(2,1)}), bf16[32,8,1,256]{3,1,2,0:T(8,128)(2,1)S(1)}, u32[]{:S(2)}, u32[]{:S(2)}) async-start(bf16[32,8,1,256]{3,1,2,0:T(8,128)(2,1)} %bitcast.26), calls=%async_computation | async-start | bytes 262144 | tf_op jit(solution)/shard_map/all_to_all | solution.py:94
  347.9 1.7 sort.32
  349.6 13.7 %all-to-all-done = bf16[32,8,1,256]{3,1,2,0:T(8,128)(2,1)S(1)} async-done(((bf16[32,8,1,256]{3,1,2,0:T(8,128)(2,1)}), bf16[32,8,1,256]{3,1,2,0:T(8,128)(2,1)S(1)}, u32[]{:S(2)}, u32[]{:S(2)}) %all-to-all-start) | async-done | bytes 131104 | tf_op jit(solution)/shard_map/all_to_all | solution.py:94
  364.6 69.8 %all-reduce.3.cloned.1.call-done = bf16[256,2048]{1,0:T(8,128)(2,1)} async-done(((bf16[256,2048]{1,0:T(8,128)(2,1)}), bf16[256,2048]{1,0:T(8,128)(2,1)}) %all-reduce.3.cloned.1.call-update) | async-done | bytes 1048592 | tf_op jit(solution)/shard_map/psum | solution.py:139
  434.3 1.5 fusion.24
  435.9 2.6 fusion.27
  (194 shorter events, 48.0 us)
Async XLA Ops:
  7.2 79.6 %copy-start = (bf16[2048,1,384]{2,0,1:T(8,128)(2,1)S(1)}, bf16[2048,1,384]{2,0,1:T(8,128)(2,1)}, u32[]{:S(2)}) copy-start(bf16[2048,1,384]{2,0,1:T(8,128)(2,1)} %param.19) | copy-start | bytes 4718596
  7.2 191.9 %all-gather.3.cloned.1.call-start = ((), (), s32[]{:S(2)}) async-start(), calls=%async_computation.2 | async-start | bytes 2162688 | tf_op jit(solution)/shard_map/all_gather | solution.py:124
  10.4 78.3 %copy-start.8 = (bf16[16,3,16,1,128]{4,2,3,1,0:T(8,128)(2,1)S(1)}, bf16[16,3,16,1,128]{4,2,3,1,0:T(8,128)(2,1)}, u32[]{:S(2)}) copy-start(bf16[16,3,16,1,128]{4,2,3,1,0:T(8,128)(2,1)} %param.21) | copy-start | bytes 589828
  88.7 36.0 %copy-start.6 = (f32[1,128]{1,0:T(1,128)S(1)}, f32[1,128]{1,0:T(1,128)}, u32[]{:S(2)}) copy-start(f32[1,128]{1,0:T(1,128)} %param.23) | copy-start | bytes 1540
  88.7 36.0 %copy-start.7 = (f32[1,128]{1,0:T(1,128)S(1)}, f32[1,128]{1,0:T(1,128)}, u32[]{:S(2)}) copy-start(f32[1,128]{1,0:T(1,128)} %param.22) | copy-start | bytes 1540
  126.8 143.8 %all-gather.5.cloned.1.call-start = ((), (), s32[]{:S(2)}) async-start(), calls=%async_computation.3 | async-start | bytes 2162688 | tf_op jit(solution)/shard_map/all_gather | solution.py:125
  127.5 306.8 %all-reduce.3.cloned.1.call-start = ((), (), s32[]{:S(2)}) async-start(), calls=%async_computation.4 | async-start | bytes 2097152 | tf_op jit(solution)/shard_map/psum | solution.py:139
  270.6 47.3 %copy-start.4 = (bf16[1,128,2048]{2,1,0:T(8,128)(2,1)S(1)}, bf16[1,128,2048]{2,1,0:T(8,128)(2,1)}, u32[]{:S(2)}) copy-start(bf16[1,128,2048]{2,1,0:T(8,128)(2,1)} %param.24) | copy-start | bytes 1572868
  317.9 1.5 copy-start.1
  317.9 13.1 %copy-start.3 = (bf16[256,1,128]{2,0,1:T(8,128)(2,1)S(1)}, bf16[256,1,128]{2,0,1:T(8,128)(2,1)}, u32[]{:S(2)}) copy-start(bf16[256,1,128]{2,0,1:T(8,128)(2,1)} %get-tuple-element.260) | copy-start | bytes 196612
  319.4 116.5 %copy-start.2 = (bf16[256,2048]{1,0:T(8,128)(2,1)S(1)}, bf16[256,2048]{1,0:T(8,128)(2,1)}, u32[]{:S(2)}) copy-start(bf16[256,2048]{1,0:T(8,128)(2,1)} %param.14) | copy-start | bytes 3145732
  319.4 116.5 %copy-start.5 = (f32[2048]{0:T(1024)S(1)}, f32[2048]{0:T(1024)}, u32[]{:S(2)}) copy-start(f32[2048]{0:T(1024)} %param.25) | copy-start | bytes 24580
  322.5 19.7 %all-to-all-start.1 = ((s32[32,1,1]{2,1,0:T(1,128)}), s32[32,1,1]{2,1,0:T(1,128)S(1)}, u32[]{:S(2)}, u32[]{:S(2)}) async-start(s32[32,1,1]{2,1,0:T(1,128)} %copy.31), calls=%async_computation.1 | async-start | bytes 32768 | tf_op jit(solution)/shard_map/all_to_all | solution.py:95
  342.2 21.1 %all-to-all-start = ((bf16[32,8,1,256]{3,1,2,0:T(8,128)(2,1)}), bf16[32,8,1,256]{3,1,2,0:T(8,128)(2,1)S(1)}, u32[]{:S(2)}, u32[]{:S(2)}) async-start(bf16[32,8,1,256]{3,1,2,0:T(8,128)(2,1)} %bitcast.26), calls=%async_computation | async-start | bytes 262144 | tf_op jit(solution)/shard_map/all_to_all | solution.py:94
Sparse Core Ops, SparseCore 0:
  126.9 72.1 all-gather.2
  201.8 68.8 all-gather.4
  319.5 114.7 all-reduce.2
where the time goes:
time: 446 us; the launch traced here: 445 us
  waiting for transfers between devices  237 us (53%)
  blocking collectives  110 us (25%)
  matrix products  46.3 us (10%)
  other arithmetic  19.1 us (4%)
  between operations  14 us (3%)
  starting transfers between devices  13.6 us (3%)
    psum x1, blocking collectives, shards(): low = lax.psum(partial_low.astype(jnp.bfloat16), 'gy')  74.6 us
    all_gather x1, waiting for transfers between devices, shards(): values = lax.all_gather(value_b, 'gx', axis=0, tiled=True)  71.5 us
    all_gather x1, waiting for transfers between devices, shards(): key_vectors = lax.all_gather(key_b, 'gx', axis=0, tiled=True)  71.4 us
    psum x1, waiting for transfers between devices, shards(): lax.psum(partial_out.astype(jnp.bfloat16), 'gy').astype(jnp.float32)  69.8 us
    psum x1, blocking collectives, shards(): lax.psum((jnp.sum(query * query, axis=(1, 2)), jnp.sum(key_raw * key_raw,...  35.5 us
    dot_general x16, matrix products, attend(): jnp.einsum('htk,khe->hte', weights.astype(jnp.bfloat16), values, preferre...  21.9 us
    dot_general x16, matrix products, attend(): jnp.einsum('the,khe->htk', query_b, key_vectors, preferred_element_type=j...  19 us
    all_to_all x1, waiting for transfers between devices, shards(): lax.all_to_all(pages[order], 'gx', split_axis=0, concat_axis=0, tiled=True)  13.7 us
  transfers between devices with their start and end apart: 5, of which 5 were waited for; matrix products, arithmetic and copies ran while one was open for 2% of the time, Pallas kernels for 0%

commit v1 on v0

--- a/solution.py
+++ b/solution.py
@@ -1,3 +1,4 @@
+import functools
 import jax
 import jax.numpy as jnp
 from jax import lax
@@ -7,6 +8,16 @@
 HEAD_SIZE = 128
 ADAPTER_RANK = 16
 PAGE = 8
+
+
+def answer_terms(panel, dim_i):
+    return jnp.concatenate(
+        lax.all_to_all(jnp.stack([panel for _ in range(lax.axis_size("gx"))], axis=0), "gx", 0, 0),
+        dim_i,
+    )
+
+
+list_rails = functools.partial(answer_terms, dim_i=0)
 
 
 def request_of(rows, ends):
@@ -122,7 +133,7 @@
         jnp.zeros((heads_here, count, HEAD_SIZE), jnp.float32),
     )
     key_vectors = lax.all_gather(key_b, "gx", axis=0, tiled=True)
-    values = lax.all_gather(value_b, "gx", axis=0, tiled=True)
+    values = list_rails(value_b)
     size = key_vectors.shape[0]
     block = 512
 

time: 446 us -> 423 us (0.948)
  waiting for transfers between devices: 237 us -> 200 us
  starting transfers between devices: 13.6 us -> 25.9 us
    all_gather x1 -> x0, waiting for transfers between devices: 71.5 us -> none  [shards(): values = lax.all_gather(value_b, 'gx', axis=0, tiled=True)]
    all_gather x1, waiting for transfers between devices: 71.4 us -> 105 us  [shards(): key_vectors = lax.all_gather(key_b, 'gx', axis=0, tiled=True)]
    all_to_all x0 -> x1, starting transfers between devices: none -> 15.4 us  [answer_terms(): lax.all_to_all(jnp.stack([panel for _ in range(lax.axis_size('gx'))], axi...]
    all_to_all x0 -> x1, waiting for transfers between devices: none -> 4.63 us  [answer_terms(): lax.all_to_all(jnp.stack([panel for _ in range(lax.axis_size('gx'))], axi...]
where the time goes in v1:
time: 423 us; the launch traced here: 422 us
  waiting for transfers between devices  200 us (47%)
  blocking collectives  110 us (26%)
  matrix products  46.3 us (11%)
  starting transfers between devices  25.9 us (6%)
  other arithmetic  18.5 us (4%)
  between operations  14.3 us (3%)
  local copies, waits for them, and re-layouts  5.73 us (1%)
    all_gather x1, waiting for transfers between devices, shards(): key_vectors = lax.all_gather(key_b, 'gx', axis=0, tiled=True)  105 us
    psum x1, blocking collectives, shards(): low = lax.psum(partial_low.astype(jnp.bfloat16), 'gy')  74.6 us
    psum x1, waiting for transfers between devices, shards(): lax.psum(partial_out.astype(jnp.bfloat16), 'gy').astype(jnp.float32)  67.6 us
    psum x1, blocking collectives, shards(): lax.psum((jnp.sum(query * query, axis=(1, 2)), jnp.sum(key_raw * key_raw,...  35.5 us
    dot_general x16, matrix products, attend(): jnp.einsum('htk,khe->hte', weights.astype(jnp.bfloat16), values, preferre...  21.9 us
    dot_general x16, matrix products, attend(): jnp.einsum('the,khe->htk', query_b, key_vectors, preferred_element_type=j...  19 us
    all_to_all x1, starting transfers between devices, answer_terms(): lax.all_to_all(jnp.stack([panel for _ in range(lax.axis_size('gx'))], axi...  15.4 us
    all_to_all x1, waiting for transfers between devices, shards(): lax.all_to_all(pages[order], 'gx', split_axis=0, concat_axis=0, tiled=True)  13.7 us
  transfers between devices with their start and end apart: 5, of which 5 were waited for; matrix products, arithmetic and copies ran while one was open for 2% of the time, Pallas kernels for 0%

profile of v1, /device:TPU:32, one launch (start us, length us, event | category | flops | bytes accessed | tf_op | source)
XLA Modules:
  0.0 422.2 jit_solution(15079948194238390208)
XLA Ops:
  10.4 1.7 fusion.33
  12.1 74.6 %psum.28 = bf16[256,3,16]{0,2,1:T(8,128)(2,1)S(1)} all-reduce(bf16[256,3,16]{0,2,1:T(8,128)(2,1)S(1)} %bitcast.117), channel_id=1, replica_groups=mesh['gx'=32,'gy'=16] {'gy'}, use_global_device_ids=true, to_apply=%region_4.5 | all-reduce | flops 12288 | bytes 49152 | tf_op jit(solution)/shard_map/psum | solution.py:75
  86.7 1.9 fusion.30
  89.2 35.5 %all-reduce = (f32[256]{0:T(256)S(1)}, f32[256]{0:T(256)S(1)}) all-reduce(f32[256]{0:T(256)S(1)} %get-tuple-element.231, f32[256]{0:T(256)S(1)} %get-tuple-element.230), channel_id=1, replica_groups=mesh['gx'=32,'gy'=16] {'gy'}, use_global_device_ids=true, to_apply=%region_6.7 | all-reduce | flops 512 | bytes 4096 | tf_op jit(solution)/shard_map/psum | solution.py:88
  124.8 1.8 stack.2
  126.6 15.4 %all-to-all-start = ((bf16[32,256,1,128]{3,1,2,0:T(8,128)(2,1)}), bf16[32,256,1,128]{3,1,2,0:T(8,128)(2,1)}, u32[]{:S(2)}, u32[]{:S(2)}) async-start(bf16[32,256,1,128]{3,1,2,0:T(8,128)(2,1)} %stack.2), calls=%async_computation | async-start | bytes 4194304 | tf_op jit(solution)/shard_map/all_to_all | solution.py:15
  143.7 104.6 %all-gather.2.cloned.1.call-done = bf16[8192,1,128]{2,0,1:T(8,128)(2,1)} async-done(((bf16[256,1,128]{2,0,1:T(8,128)(2,1)}), bf16[8192,1,128]{2,0,1:T(8,128)(2,1)}) %all-gather.2.cloned.1.call-update) | async-done | bytes 2097168 | tf_op jit(solution)/shard_map/all_gather | solution.py:135
  248.3 4.6 %all-to-all-done = bf16[32,256,1,128]{3,1,2,0:T(8,128)(2,1)} async-done(((bf16[32,256,1,128]{3,1,2,0:T(8,128)(2,1)}), bf16[32,256,1,128]{3,1,2,0:T(8,128)(2,1)}, u32[]{:S(2)}, u32[]{:S(2)}) %all-to-all-start) | async-done | bytes 2097184 | tf_op jit(solution)/shard_map/all_to_all | solution.py:15
  252.9 47.3 %while.18 = (s32[]{:T(128)}, f32[1,256]{1,0:T(1,128)S(1)}, f32[1,256]{1,0:T(1,128)S(1)}, f32[1,256,128]{2,1,0:T(8,128)S(1)}, s32[256]{0:T(256)S(1)}, /*index=5*/...) while((s32[]{:T(128)}, f32[1,256]{1,0:T(1,128)S(1)}, ...), condition=%wide.region_14.15_spmd.clone, body=%wide.region_10.14_spmd.clone.sunk | while | flops 69574144 | bytes 2204895 | solution.py:147
  254.5 1.4 fusion.75
  260.4 1.4 fusion.75
  266.3 1.4 fusion.75
  272.2 1.4 fusion.75
  278.1 1.4 fusion.75
  300.2 1.5 convolution_convert_fusion
  301.7 1.6 sort.31
  304.7 5.4 %all-to-all-start.2 = ((s32[32,1,1]{2,1,0:T(1,128)}), s32[32,1,1]{2,1,0:T(1,128)S(1)}, u32[]{:S(2)}, u32[]{:S(2)}) async-start(s32[32,1,1]{2,1,0:T(1,128)} %copy.30), calls=%async_computation.2 | async-start | bytes 32768 | tf_op jit(solution)/shard_map/all_to_all | solution.py:106
  311.4 9.8 %all-to-all-done.2 = s32[32,1,1]{2,1,0:T(1,128)S(1)} async-done(((s32[32,1,1]{2,1,0:T(1,128)}), s32[32,1,1]{2,1,0:T(1,128)S(1)}, u32[]{:S(2)}, u32[]{:S(2)}) %all-to-all-start.2) | async-done | bytes 160 | tf_op jit(solution)/shard_map/all_to_all | solution.py:106
  321.2 5.0 %all-to-all-start.1 = ((bf16[32,8,1,256]{3,1,2,0:T(8,128)(2,1)}), bf16[32,8,1,256]{3,1,2,0:T(8,128)(2,1)S(1)}, u32[]{:S(2)}, u32[]{:S(2)}) async-start(bf16[32,8,1,256]{3,1,2,0:T(8,128)(2,1)} %bitcast.28), calls=%async_computation.1 | async-start | bytes 262144 | tf_op jit(solution)/shard_map/all_to_all | solution.py:105
  326.9 1.7 sort.32
  328.6 13.7 %all-to-all-done.1 = bf16[32,8,1,256]{3,1,2,0:T(8,128)(2,1)S(1)} async-done(((bf16[32,8,1,256]{3,1,2,0:T(8,128)(2,1)}), bf16[32,8,1,256]{3,1,2,0:T(8,128)(2,1)S(1)}, u32[]{:S(2)}, u32[]{:S(2)}) %all-to-all-start.1) | async-done | bytes 131104 | tf_op jit(solution)/shard_map/all_to_all | solution.py:105
  343.6 67.6 %all-reduce.3.cloned.1.call-done = bf16[256,2048]{1,0:T(8,128)(2,1)} async-done(((bf16[256,2048]{1,0:T(8,128)(2,1)}), bf16[256,2048]{1,0:T(8,128)(2,1)}) %all-reduce.3.cloned.1.call-update) | async-done | bytes 1048592 | tf_op jit(solution)/shard_map/psum | solution.py:150
  411.1 1.5 fusion.24
  412.7 2.6 fusion.27
  (192 shorter events, 49.5 us)
Async XLA Ops:
  7.2 79.6 %copy-start = (bf16[2048,1,384]{2,0,1:T(8,128)(2,1)S(1)}, bf16[2048,1,384]{2,0,1:T(8,128)(2,1)}, u32[]{:S(2)}) copy-start(bf16[2048,1,384]{2,0,1:T(8,128)(2,1)} %param.19) | copy-start | bytes 4718596
  10.4 78.3 %copy-start.7 = (bf16[16,3,16,1,128]{4,2,3,1,0:T(8,128)(2,1)S(1)}, bf16[16,3,16,1,128]{4,2,3,1,0:T(8,128)(2,1)}, u32[]{:S(2)}) copy-start(bf16[16,3,16,1,128]{4,2,3,1,0:T(8,128)(2,1)} %param.21) | copy-start | bytes 589828
  88.7 36.0 %copy-start.5 = (f32[1,128]{1,0:T(1,128)S(1)}, f32[1,128]{1,0:T(1,128)}, u32[]{:S(2)}) copy-start(f32[1,128]{1,0:T(1,128)} %param.23) | copy-start | bytes 1540
  88.7 36.0 %copy-start.6 = (f32[1,128]{1,0:T(1,128)S(1)}, f32[1,128]{1,0:T(1,128)}, u32[]{:S(2)}) copy-start(f32[1,128]{1,0:T(1,128)} %param.22) | copy-start | bytes 1540
  126.6 126.2 %all-to-all-start = ((bf16[32,256,1,128]{3,1,2,0:T(8,128)(2,1)}), bf16[32,256,1,128]{3,1,2,0:T(8,128)(2,1)}, u32[]{:S(2)}, u32[]{:S(2)}) async-start(bf16[32,256,1,128]{3,1,2,0:T(8,128)(2,1)} %stack.2), calls=%async_computation | async-start | bytes 4194304 | tf_op jit(solution)/shard_map/all_to_all | solution.py:15
  142.1 106.2 %all-gather.2.cloned.1.call-start = ((), (), s32[]{:S(2)}) async-start(), calls=%async_computation.3 | async-start | bytes 2162688 | tf_op jit(solution)/shard_map/all_gather | solution.py:135
  143.5 267.6 %all-reduce.3.cloned.1.call-start = ((), (), s32[]{:S(2)}) async-start(), calls=%async_computation.4 | async-start | bytes 2097152 | tf_op jit(solution)/shard_map/psum | solution.py:150
  252.9 47.3 %copy-start.3 = (bf16[1,128,2048]{2,1,0:T(8,128)(2,1)S(1)}, bf16[1,128,2048]{2,1,0:T(8,128)(2,1)}, u32[]{:S(2)}) copy-start(bf16[1,128,2048]{2,1,0:T(8,128)(2,1)} %param.24) | copy-start | bytes 1572868
  300.1 1.5 copy-start.1
  301.6 111.0 %copy-start.2 = (bf16[256,2048]{1,0:T(8,128)(2,1)S(1)}, bf16[256,2048]{1,0:T(8,128)(2,1)}, u32[]{:S(2)}) copy-start(bf16[256,2048]{1,0:T(8,128)(2,1)} %param.14) | copy-start | bytes 3145732
  301.6 111.0 %copy-start.4 = (f32[2048]{0:T(1024)S(1)}, f32[2048]{0:T(1024)}, u32[]{:S(2)}) copy-start(f32[2048]{0:T(1024)} %param.25) | copy-start | bytes 24580
  304.7 16.6 %all-to-all-start.2 = ((s32[32,1,1]{2,1,0:T(1,128)}), s32[32,1,1]{2,1,0:T(1,128)S(1)}, u32[]{:S(2)}, u32[]{:S(2)}) async-start(s32[32,1,1]{2,1,0:T(1,128)} %copy.30), calls=%async_computation.2 | async-start | bytes 32768 | tf_op jit(solution)/shard_map/all_to_all | solution.py:106
  321.2 21.1 %all-to-all-start.1 = ((bf16[32,8,1,256]{3,1,2,0:T(8,128)(2,1)}), bf16[32,8,1,256]{3,1,2,0:T(8,128)(2,1)S(1)}, u32[]{:S(2)}, u32[]{:S(2)}) async-start(bf16[32,8,1,256]{3,1,2,0:T(8,128)(2,1)} %bitcast.28), calls=%async_computation.1 | async-start | bytes 262144 | tf_op jit(solution)/shard_map/all_to_all | solution.py:105
Sparse Core Ops, SparseCore 0:
  145.6 102.6 all-gather.1
  301.8 109.3 all-reduce.2
